TPU v7x, 512 devices: a whole 4x8x8 slice. The times are simulated.
512 devices in a mesh: space: 64 (over z, x, y_lo), sta: 8 (over y_hi, core).
Axes of the slice: x: 4, y: 8 (y_hi: 4, y_lo: 2; y = y_hi * 2 + y_lo), z: 8, core: 2. Of those that a mesh axis runs over, the one named last changes fastest.
Arguments:
- coarse_times: float32 [16, 320, 32, 128], P('sta', 'space'), as said below
- model_map: int32 [320, 32, 128], P('space'), may hold values from 0 to 63
- slowness: float32 [64], replicated, may hold values from 0.12 to 0.3
- picks: float32 [256, 16], replicated
- pick_mask: int32 [256, 16], replicated, may hold values from 0 to 1, as said below
Outputs:
- refined: float32 [16, 320, 32, 128], P(None, 'space', 'sta')
- density: float32 [256, 320, 32, 128], P(None, 'space', 'sta')
Inputs may be any that keep to these rules, and one draw needn't show every extreme that they name: `pick_mask`: each event has at least 4 stations with a pick. `coarse_times`: zero at each station's own cell and positive elsewhere.
All inputs are finite; a program needn't handle non-finite values.
Results may differ from a plain program's by a relative error of at most 0.0003.
Values sent between devices are 32-bit elements; how exact they have to be, the bound alone decides.
A program may use at most 64 MiB of HBM per device.

v0:
```python
import jax
import jax.numpy as jnp
from jax import lax
from jax.sharding import PartitionSpec as P

ROUNDS = 12
BIG = 1000000.0
pick_sigma = 0.25
grid_step = 1.0
block_events = 32


def extended_2(block, sides, width):
    for axis, dim in sides:
        count = lax.axis_size(axis)
        forward = [(i, i + 1) for i in range(count - 1)]
        backward = [(target, source) for source, target in forward]
        low = lax.ppermute(
            lax.slice_in_dim(block, block.shape[dim] - width, None, axis=dim), axis, forward
        )
        high = lax.ppermute(lax.slice_in_dim(block, 0, width, axis=dim), axis, backward)
        block = jnp.concatenate([low, block, high], axis=dim)
    return block


def godunov(near_one, near_two, near_three, speed):
    lowest = jnp.minimum(jnp.minimum(near_one, near_two), near_three)
    highest = jnp.maximum(jnp.maximum(near_one, near_two), near_three)
    middle = jnp.maximum(
        jnp.minimum(near_one, near_two), jnp.minimum(jnp.maximum(near_one, near_two), near_three)
    )
    gap_mid = middle - lowest
    gap_high = highest - lowest
    two_sided = 0.5 * (
        gap_mid + jnp.sqrt(jnp.maximum(2.0 * speed * speed - gap_mid * gap_mid, 0.0))
    )
    gap_sum = gap_mid + gap_high
    squares = gap_mid * gap_mid + gap_high * gap_high - speed * speed
    three_sided = (gap_sum + jnp.sqrt(jnp.maximum(gap_sum * gap_sum - 3.0 * squares, 0.0))) / 3.0
    increase = jnp.where(
        speed <= gap_mid, speed, jnp.where(two_sided <= gap_high, two_sided, three_sided)
    )
    return lowest + increase


def relax(extended, speed):
    centre = extended[:, 1:-1]
    along_x = jnp.minimum(extended[:, :-2], extended[:, 2:])
    padded = jnp.pad(centre, ((0, 0), (0, 0), (1, 1), (1, 1)), constant_values=BIG)
    along_y = jnp.minimum(padded[:, :, :-2, 1:-1], padded[:, :, 2:, 1:-1])
    along_z = jnp.minimum(padded[:, :, 1:-1, :-2], padded[:, :, 1:-1, 2:])
    return jnp.minimum(centre, godunov(along_x, along_y, along_z, speed[None]))


def close_rims(extended, rim_width, at_lower, at_upper):
    cell_count = extended.shape[1]
    position = lax.broadcasted_iota(jnp.int32, (1, cell_count, 1, 1), 1)
    outside = (position < rim_width) & at_lower | (position >= cell_count - rim_width) & at_upper
    return jnp.where(outside, BIG, extended)


def misfit_block(event_pair, flat_tables):
    arrivals, observed = event_pair
    pick_count = jnp.sum(observed, 1)
    residual = arrivals[:, :, None] - flat_tables[None]
    anchor_shift = jnp.sum(observed[:, :, None] * residual, 1) / pick_count[:, None]
    deviation = residual - anchor_shift[:, None, :]
    return jnp.sum(observed[:, :, None] * deviation * deviation, 1)


def body(coarse_times, model_map, slowness, picks, pick_mask):
    levels = lax.broadcasted_iota(jnp.int32, (slowness.shape[0], 1, 1, 1), 0)
    speed = grid_step * jnp.sum(
        jnp.where(model_map[None] == levels, slowness[:, None, None, None], 0.0), 0
    )
    position_space = lax.axis_index("space")
    devices_space = lax.axis_size("space")
    at_lower = position_space == 0
    at_upper = position_space == devices_space - 1
    tables = coarse_times

    def one_round(round_index, tables):
        extended = extended_2(tables, (("space", 1),), 1)
        return relax(close_rims(extended, 1, at_lower, at_upper), speed)

    tables = lax.fori_loop(0, ROUNDS, one_round, tables)
    refined = lax.all_to_all(tables, "sta", split_axis=2, concat_axis=0, tiled=True)
    stations = refined.shape[0]
    flat_tables = refined.reshape(stations, -1)
    observed = pick_mask.astype(jnp.float32)
    blocks = lax.map(
        lambda event_pair: misfit_block(event_pair, flat_tables),
        (picks.reshape(-1, block_events, stations), observed.reshape(-1, block_events, stations)),
    )
    score = -0.5 * blocks.reshape(picks.shape[0], -1) / (pick_sigma * pick_sigma)
    local_top = jnp.max(score, 1)
    top_score = lax.pmax(local_top, ("space", "sta"))
    cell_weights = jnp.exp(score - top_score[:, None])
    mass_sum = lax.psum(jnp.sum(cell_weights, 1), ("space", "sta"))
    density = cell_weights / mass_sum[:, None]
    density = density.reshape(picks.shape[0], refined.shape[1], refined.shape[2], refined.shape[3])
    return (refined, density)


def solution(mesh):
    placed = (P("sta", "space", None, None), P("space", None, None), P(), P(), P())
    return jax.shard_map(
        body,
        mesh=mesh,
        in_specs=placed,
        out_specs=(P(None, "space", "sta", None), P(None, "space", "sta", None)),
        check_vma=False,
    )
```

profile of v0, /device:TPU:1, one launch (start us, length us, event | category | flops | bytes accessed | tf_op | source)
XLA Modules:
  0.0 400.3 jit_solution(15108687910519187585)
XLA Ops:
  0.6 0.9 copy.54
  1.5 1.5 select_reduce_fusion
  3.1 96.4 %while.22 = (s32[]{:T(128)}, f32[2,5,32,128]{3,2,1,0:T(8,128)S(1)}, pred[]{:T(512)}, pred[]{:T(512)}, f32[5,32,128]{2,1,0:T(8,128)S(1)}, /*index=5*/f32[1,5,32,128]{3,2,1,0:T(8,128)S(1)}, s32[]{:T(128)}) while((s32[]{:T(128)}, f32[2,5,32,128]{3,2,1,0:T(8,128)S(1)}, pred[]{:T(512)}, pred[]{:T(512)}, f32[5,32,128]{2,1,0:T(8,128)S(1)}, ...), condition=%wide.region_2.3_spmd, body=%wide.region_1.2_spmd.sunk | while | flops 1523749 | bytes 2244781 | solution.py:86
  3.1 1.3 collective-permute-start
  4.4 4.6 %collective-permute-start.1 = (f32[2,1,32,128]{3,2,1,0:T(8,128)S(1)}, f32[2,1,32,128]{3,2,1,0:T(8,128)S(1)}, u32[]{:S(2)}, u32[]{:S(2)}) collective-permute-start(f32[2,1,32,128]{3,2,1,0:T(8,128)S(1)} %get-tuple-element.226), channel_id=1, source_target_pairs={{0,8},{8,16},{16,24},{24,32},{32,40},{40,48},{48,56},{56,64},{64,7... | collective-permute-start | bytes 98312 | tf_op jit(solution)/shard_map/while/body/eval_jaxpr/ppermute | solution.py:18
  9.1 1.0 collective-permute-done.1
  10.6 1.3 collective-permute-start
  11.9 4.9 %collective-permute-start.1 = (f32[2,1,32,128]{3,2,1,0:T(8,128)S(1)}, f32[2,1,32,128]{3,2,1,0:T(8,128)S(1)}, u32[]{:S(2)}, u32[]{:S(2)}) collective-permute-start(f32[2,1,32,128]{3,2,1,0:T(8,128)S(1)} %get-tuple-element.226), channel_id=1, source_target_pairs={{0,8},{8,16},{16,24},{24,32},{32,40},{40,48},{48,56},{56,64},{64,7... | collective-permute-start | bytes 98312 | tf_op jit(solution)/shard_map/while/body/eval_jaxpr/ppermute | solution.py:18
  16.8 1.0 collective-permute-done.1
  18.2 1.3 collective-permute-start
  19.5 5.2 %collective-permute-start.1 = (f32[2,1,32,128]{3,2,1,0:T(8,128)S(1)}, f32[2,1,32,128]{3,2,1,0:T(8,128)S(1)}, u32[]{:S(2)}, u32[]{:S(2)}) collective-permute-start(f32[2,1,32,128]{3,2,1,0:T(8,128)S(1)} %get-tuple-element.226), channel_id=1, source_target_pairs={{0,8},{8,16},{16,24},{24,32},{32,40},{40,48},{48,56},{56,64},{64,7... | collective-permute-start | bytes 98312 | tf_op jit(solution)/shard_map/while/body/eval_jaxpr/ppermute | solution.py:18
  24.8 1.0 collective-permute-done.1
  26.2 1.3 collective-permute-start
  27.5 5.2 %collective-permute-start.1 = (f32[2,1,32,128]{3,2,1,0:T(8,128)S(1)}, f32[2,1,32,128]{3,2,1,0:T(8,128)S(1)}, u32[]{:S(2)}, u32[]{:S(2)}) collective-permute-start(f32[2,1,32,128]{3,2,1,0:T(8,128)S(1)} %get-tuple-element.226), channel_id=1, source_target_pairs={{0,8},{8,16},{16,24},{24,32},{32,40},{40,48},{48,56},{56,64},{64,7... | collective-permute-start | bytes 98312 | tf_op jit(solution)/shard_map/while/body/eval_jaxpr/ppermute | solution.py:18
  32.7 1.0 collective-permute-done.1
  34.2 1.3 collective-permute-start
  35.5 5.2 %collective-permute-start.1 = (f32[2,1,32,128]{3,2,1,0:T(8,128)S(1)}, f32[2,1,32,128]{3,2,1,0:T(8,128)S(1)}, u32[]{:S(2)}, u32[]{:S(2)}) collective-permute-start(f32[2,1,32,128]{3,2,1,0:T(8,128)S(1)} %get-tuple-element.226), channel_id=1, source_target_pairs={{0,8},{8,16},{16,24},{24,32},{32,40},{40,48},{48,56},{56,64},{64,7... | collective-permute-start | bytes 98312 | tf_op jit(solution)/shard_map/while/body/eval_jaxpr/ppermute | solution.py:18
  40.7 1.0 collective-permute-done.1
  42.1 1.3 collective-permute-start
  43.4 5.2 %collective-permute-start.1 = (f32[2,1,32,128]{3,2,1,0:T(8,128)S(1)}, f32[2,1,32,128]{3,2,1,0:T(8,128)S(1)}, u32[]{:S(2)}, u32[]{:S(2)}) collective-permute-start(f32[2,1,32,128]{3,2,1,0:T(8,128)S(1)} %get-tuple-element.226), channel_id=1, source_target_pairs={{0,8},{8,16},{16,24},{24,32},{32,40},{40,48},{48,56},{56,64},{64,7... | collective-permute-start | bytes 98312 | tf_op jit(solution)/shard_map/while/body/eval_jaxpr/ppermute | solution.py:18
  48.7 1.0 collective-permute-done.1
  50.1 1.3 collective-permute-start
  51.4 5.2 %collective-permute-start.1 = (f32[2,1,32,128]{3,2,1,0:T(8,128)S(1)}, f32[2,1,32,128]{3,2,1,0:T(8,128)S(1)}, u32[]{:S(2)}, u32[]{:S(2)}) collective-permute-start(f32[2,1,32,128]{3,2,1,0:T(8,128)S(1)} %get-tuple-element.226), channel_id=1, source_target_pairs={{0,8},{8,16},{16,24},{24,32},{32,40},{40,48},{48,56},{56,64},{64,7... | collective-permute-start | bytes 98312 | tf_op jit(solution)/shard_map/while/body/eval_jaxpr/ppermute | solution.py:18
  56.6 1.0 collective-permute-done.1
  58.1 1.3 collective-permute-start
  59.4 5.2 %collective-permute-start.1 = (f32[2,1,32,128]{3,2,1,0:T(8,128)S(1)}, f32[2,1,32,128]{3,2,1,0:T(8,128)S(1)}, u32[]{:S(2)}, u32[]{:S(2)}) collective-permute-start(f32[2,1,32,128]{3,2,1,0:T(8,128)S(1)} %get-tuple-element.226), channel_id=1, source_target_pairs={{0,8},{8,16},{16,24},{24,32},{32,40},{40,48},{48,56},{56,64},{64,7... | collective-permute-start | bytes 98312 | tf_op jit(solution)/shard_map/while/body/eval_jaxpr/ppermute | solution.py:18
  64.6 1.0 collective-permute-done.1
  66.0 1.3 collective-permute-start
  67.3 5.3 %collective-permute-start.1 = (f32[2,1,32,128]{3,2,1,0:T(8,128)S(1)}, f32[2,1,32,128]{3,2,1,0:T(8,128)S(1)}, u32[]{:S(2)}, u32[]{:S(2)}) collective-permute-start(f32[2,1,32,128]{3,2,1,0:T(8,128)S(1)} %get-tuple-element.226), channel_id=1, source_target_pairs={{0,8},{8,16},{16,24},{24,32},{32,40},{40,48},{48,56},{56,64},{64,7... | collective-permute-start | bytes 98312 | tf_op jit(solution)/shard_map/while/body/eval_jaxpr/ppermute | solution.py:18
  72.6 1.0 collective-permute-done.1
  74.1 1.3 collective-permute-start
  75.4 5.3 %collective-permute-start.1 = (f32[2,1,32,128]{3,2,1,0:T(8,128)S(1)}, f32[2,1,32,128]{3,2,1,0:T(8,128)S(1)}, u32[]{:S(2)}, u32[]{:S(2)}) collective-permute-start(f32[2,1,32,128]{3,2,1,0:T(8,128)S(1)} %get-tuple-element.226), channel_id=1, source_target_pairs={{0,8},{8,16},{16,24},{24,32},{32,40},{40,48},{48,56},{56,64},{64,7... | collective-permute-start | bytes 98312 | tf_op jit(solution)/shard_map/while/body/eval_jaxpr/ppermute | solution.py:18
  80.8 1.0 collective-permute-done.1
  82.2 1.3 collective-permute-start
  83.5 5.2 %collective-permute-start.1 = (f32[2,1,32,128]{3,2,1,0:T(8,128)S(1)}, f32[2,1,32,128]{3,2,1,0:T(8,128)S(1)}, u32[]{:S(2)}, u32[]{:S(2)}) collective-permute-start(f32[2,1,32,128]{3,2,1,0:T(8,128)S(1)} %get-tuple-element.226), channel_id=1, source_target_pairs={{0,8},{8,16},{16,24},{24,32},{32,40},{40,48},{48,56},{56,64},{64,7... | collective-permute-start | bytes 98312 | tf_op jit(solution)/shard_map/while/body/eval_jaxpr/ppermute | solution.py:18
  88.7 1.0 collective-permute-done.1
  90.2 1.3 collective-permute-start
  91.5 6.5 %collective-permute-start.1 = (f32[2,1,32,128]{3,2,1,0:T(8,128)S(1)}, f32[2,1,32,128]{3,2,1,0:T(8,128)S(1)}, u32[]{:S(2)}, u32[]{:S(2)}) collective-permute-start(f32[2,1,32,128]{3,2,1,0:T(8,128)S(1)} %get-tuple-element.226), channel_id=1, source_target_pairs={{0,8},{8,16},{16,24},{24,32},{32,40},{40,48},{48,56},{56,64},{64,7... | collective-permute-start | bytes 98312 | tf_op jit(solution)/shard_map/while/body/eval_jaxpr/ppermute | solution.py:18
  98.1 1.0 collective-permute-done.1
  99.5 0.8 copy.27
  100.3 20.7 %all-to-all-start = ((f32[2,5,32,128]{3,0,1,2:T(2,128)}), f32[2,5,32,128]{3,0,1,2:T(2,128)S(1)}, u32[]{:S(2)}, u32[]{:S(2)}) async-start(f32[2,5,32,128]{3,0,1,2:T(2,128)} %copy.27), calls=%async_computation | async-start | bytes 327680 | tf_op jit(solution)/shard_map/all_to_all | solution.py:87
  121.2 8.6 %all-to-all-done = f32[2,5,32,128]{3,0,1,2:T(2,128)S(1)} async-done(((f32[2,5,32,128]{3,0,1,2:T(2,128)}), f32[2,5,32,128]{3,0,1,2:T(2,128)S(1)}, u32[]{:S(2)}, u32[]{:S(2)}) %all-to-all-start) | async-done | bytes 163872 | tf_op jit(solution)/shard_map/all_to_all | solution.py:87
  130.4 26.5 %while.23 = (s32[]{:T(128)}, f32[8,32,2560]{2,1,0:T(8,128)S(1)}, f32[8,32,16]{1,0,2:T(8,128)S(1)}, f32[8,32,16]{1,0,2:T(8,128)S(1)}, f32[16,5,4,128]{3,2,1,0:T(4...) while((s32[]{:T(128)}, f32[8,32,2560]{2,1,0:T(8,128)S(1)}, f32[8,32,16]{1,0,2:T(8,128)S(1)}, ...), condition=%wide.wide.region_7.8_spmd, body=%wide.wide.region_3.7_spmd.sunk | while | flops 10404322 | bytes 2648417 | solution.py:91
  130.6 1.2 fusion.17
  131.9 1.8 fusion.18
  133.9 1.2 fusion.17
  135.3 1.8 fusion.18
  137.2 1.2 fusion.17
  138.6 1.8 fusion.18
  140.6 1.2 fusion.17
  141.9 1.8 fusion.18
  143.9 1.2 fusion.17
  145.2 1.8 fusion.18
  147.2 1.2 fusion.17
  148.5 1.8 fusion.18
  150.5 1.2 fusion.17
  151.8 1.8 fusion.18
  153.8 1.2 fusion.17
  155.1 1.8 fusion.18
  157.3 141.2 %pmax.7 = f32[256]{0:T(256)S(1)} all-reduce(f32[256]{0:T(256)S(1)} %reduce_max.12), channel_id=1, replica_groups=mesh['space'=64,'sta'=8] {'space','sta'}, use_global_device_ids=true, to_apply=%region_9.10 | all-reduce | flops 256 | bytes 2048 | tf_op jit(solution)/shard_map/pmax | solution.py:97
  298.5 2.0 exponential_reduce_fusion
  300.5 2.8 div.34
  303.4 94.4 %psum.7 = f32[256]{0:T(256)S(1)} all-reduce(f32[256]{0:T(256)S(1)} %reduce_sum.49), channel_id=1, replica_groups=mesh['space'=64,'sta'=8] {'space','sta'}, use_global_device_ids=true, to_apply=%region_11.12 | all-reduce | flops 256 | bytes 2048 | tf_op jit(solution)/shard_map/psum | solution.py:99
  397.8 2.5 exponential_divide_fusion
  (149 shorter events, 9.4 us)
Async XLA Ops:
  3.1 117.9 %copy-start.2 = (s32[256,16]{0,1:T(8,128)S(1)}, s32[256,16]{0,1:T(8,128)}, u32[]{:S(2)}) copy-start(s32[256,16]{0,1:T(8,128)} %param.13) | copy-start | bytes 49156
  3.1 118.0 %copy-start.1 = (f32[256,16]{0,1:T(8,128)S(1)}, f32[256,16]{0,1:T(8,128)}, u32[]{:S(2)}) copy-start(f32[256,16]{0,1:T(8,128)} %param.12) | copy-start | bytes 49156
  3.1 6.0 %collective-permute-start = (f32[2,1,32,128]{3,2,1,0:T(8,128)S(1)}, f32[2,1,32,128]{3,2,1,0:T(8,128)S(1)}, u32[]{:S(2)}, u32[]{:S(2)}) collective-permute-start(f32[2,1,32,128]{3,2,1,0:T(8,128)S(1)} %get-tuple-element.225), channel_id=1, source_target_pairs={{8,0},{16,8},{24,16},{32,24},{40,32},{48,40},{56,48},{64,56},{72,6... | collective-permute-start | bytes 98312 | tf_op jit(solution)/shard_map/while/body/eval_jaxpr/ppermute | solution.py:21
  4.4 5.7 %collective-permute-start.1 = (f32[2,1,32,128]{3,2,1,0:T(8,128)S(1)}, f32[2,1,32,128]{3,2,1,0:T(8,128)S(1)}, u32[]{:S(2)}, u32[]{:S(2)}) collective-permute-start(f32[2,1,32,128]{3,2,1,0:T(8,128)S(1)} %get-tuple-element.226), channel_id=1, source_target_pairs={{0,8},{8,16},{16,24},{24,32},{32,40},{40,48},{48,56},{56,64},{64,7... | collective-permute-start | bytes 98312 | tf_op jit(solution)/shard_map/while/body/eval_jaxpr/ppermute | solution.py:18
  10.6 6.2 %collective-permute-start = (f32[2,1,32,128]{3,2,1,0:T(8,128)S(1)}, f32[2,1,32,128]{3,2,1,0:T(8,128)S(1)}, u32[]{:S(2)}, u32[]{:S(2)}) collective-permute-start(f32[2,1,32,128]{3,2,1,0:T(8,128)S(1)} %get-tuple-element.225), channel_id=1, source_target_pairs={{8,0},{16,8},{24,16},{32,24},{40,32},{48,40},{56,48},{64,56},{72,6... | collective-permute-start | bytes 98312 | tf_op jit(solution)/shard_map/while/body/eval_jaxpr/ppermute | solution.py:21
  11.9 5.9 %collective-permute-start.1 = (f32[2,1,32,128]{3,2,1,0:T(8,128)S(1)}, f32[2,1,32,128]{3,2,1,0:T(8,128)S(1)}, u32[]{:S(2)}, u32[]{:S(2)}) collective-permute-start(f32[2,1,32,128]{3,2,1,0:T(8,128)S(1)} %get-tuple-element.226), channel_id=1, source_target_pairs={{0,8},{8,16},{16,24},{24,32},{32,40},{40,48},{48,56},{56,64},{64,7... | collective-permute-start | bytes 98312 | tf_op jit(solution)/shard_map/while/body/eval_jaxpr/ppermute | solution.py:18
  18.2 6.5 %collective-permute-start = (f32[2,1,32,128]{3,2,1,0:T(8,128)S(1)}, f32[2,1,32,128]{3,2,1,0:T(8,128)S(1)}, u32[]{:S(2)}, u32[]{:S(2)}) collective-permute-start(f32[2,1,32,128]{3,2,1,0:T(8,128)S(1)} %get-tuple-element.225), channel_id=1, source_target_pairs={{8,0},{16,8},{24,16},{32,24},{40,32},{48,40},{56,48},{64,56},{72,6... | collective-permute-start | bytes 98312 | tf_op jit(solution)/shard_map/while/body/eval_jaxpr/ppermute | solution.py:21
  19.5 6.2 %collective-permute-start.1 = (f32[2,1,32,128]{3,2,1,0:T(8,128)S(1)}, f32[2,1,32,128]{3,2,1,0:T(8,128)S(1)}, u32[]{:S(2)}, u32[]{:S(2)}) collective-permute-start(f32[2,1,32,128]{3,2,1,0:T(8,128)S(1)} %get-tuple-element.226), channel_id=1, source_target_pairs={{0,8},{8,16},{16,24},{24,32},{32,40},{40,48},{48,56},{56,64},{64,7... | collective-permute-start | bytes 98312 | tf_op jit(solution)/shard_map/while/body/eval_jaxpr/ppermute | solution.py:18
  26.2 6.5 %collective-permute-start = (f32[2,1,32,128]{3,2,1,0:T(8,128)S(1)}, f32[2,1,32,128]{3,2,1,0:T(8,128)S(1)}, u32[]{:S(2)}, u32[]{:S(2)}) collective-permute-start(f32[2,1,32,128]{3,2,1,0:T(8,128)S(1)} %get-tuple-element.225), channel_id=1, source_target_pairs={{8,0},{16,8},{24,16},{32,24},{40,32},{48,40},{56,48},{64,56},{72,6... | collective-permute-start | bytes 98312 | tf_op jit(solution)/shard_map/while/body/eval_jaxpr/ppermute | solution.py:21
  27.5 6.2 %collective-permute-start.1 = (f32[2,1,32,128]{3,2,1,0:T(8,128)S(1)}, f32[2,1,32,128]{3,2,1,0:T(8,128)S(1)}, u32[]{:S(2)}, u32[]{:S(2)}) collective-permute-start(f32[2,1,32,128]{3,2,1,0:T(8,128)S(1)} %get-tuple-element.226), channel_id=1, source_target_pairs={{0,8},{8,16},{16,24},{24,32},{32,40},{40,48},{48,56},{56,64},{64,7... | collective-permute-start | bytes 98312 | tf_op jit(solution)/shard_map/while/body/eval_jaxpr/ppermute | solution.py:18
  34.2 6.5 %collective-permute-start = (f32[2,1,32,128]{3,2,1,0:T(8,128)S(1)}, f32[2,1,32,128]{3,2,1,0:T(8,128)S(1)}, u32[]{:S(2)}, u32[]{:S(2)}) collective-permute-start(f32[2,1,32,128]{3,2,1,0:T(8,128)S(1)} %get-tuple-element.225), channel_id=1, source_target_pairs={{8,0},{16,8},{24,16},{32,24},{40,32},{48,40},{56,48},{64,56},{72,6... | collective-permute-start | bytes 98312 | tf_op jit(solution)/shard_map/while/body/eval_jaxpr/ppermute | solution.py:21
  35.5 6.2 %collective-permute-start.1 = (f32[2,1,32,128]{3,2,1,0:T(8,128)S(1)}, f32[2,1,32,128]{3,2,1,0:T(8,128)S(1)}, u32[]{:S(2)}, u32[]{:S(2)}) collective-permute-start(f32[2,1,32,128]{3,2,1,0:T(8,128)S(1)} %get-tuple-element.226), channel_id=1, source_target_pairs={{0,8},{8,16},{16,24},{24,32},{32,40},{40,48},{48,56},{56,64},{64,7... | collective-permute-start | bytes 98312 | tf_op jit(solution)/shard_map/while/body/eval_jaxpr/ppermute | solution.py:18
  42.1 6.5 %collective-permute-start = (f32[2,1,32,128]{3,2,1,0:T(8,128)S(1)}, f32[2,1,32,128]{3,2,1,0:T(8,128)S(1)}, u32[]{:S(2)}, u32[]{:S(2)}) collective-permute-start(f32[2,1,32,128]{3,2,1,0:T(8,128)S(1)} %get-tuple-element.225), channel_id=1, source_target_pairs={{8,0},{16,8},{24,16},{32,24},{40,32},{48,40},{56,48},{64,56},{72,6... | collective-permute-start | bytes 98312 | tf_op jit(solution)/shard_map/while/body/eval_jaxpr/ppermute | solution.py:21
  43.4 6.2 %collective-permute-start.1 = (f32[2,1,32,128]{3,2,1,0:T(8,128)S(1)}, f32[2,1,32,128]{3,2,1,0:T(8,128)S(1)}, u32[]{:S(2)}, u32[]{:S(2)}) collective-permute-start(f32[2,1,32,128]{3,2,1,0:T(8,128)S(1)} %get-tuple-element.226), channel_id=1, source_target_pairs={{0,8},{8,16},{16,24},{24,32},{32,40},{40,48},{48,56},{56,64},{64,7... | collective-permute-start | bytes 98312 | tf_op jit(solution)/shard_map/while/body/eval_jaxpr/ppermute | solution.py:18
  50.1 6.5 %collective-permute-start = (f32[2,1,32,128]{3,2,1,0:T(8,128)S(1)}, f32[2,1,32,128]{3,2,1,0:T(8,128)S(1)}, u32[]{:S(2)}, u32[]{:S(2)}) collective-permute-start(f32[2,1,32,128]{3,2,1,0:T(8,128)S(1)} %get-tuple-element.225), channel_id=1, source_target_pairs={{8,0},{16,8},{24,16},{32,24},{40,32},{48,40},{56,48},{64,56},{72,6... | collective-permute-start | bytes 98312 | tf_op jit(solution)/shard_map/while/body/eval_jaxpr/ppermute | solution.py:21
  51.4 6.2 %collective-permute-start.1 = (f32[2,1,32,128]{3,2,1,0:T(8,128)S(1)}, f32[2,1,32,128]{3,2,1,0:T(8,128)S(1)}, u32[]{:S(2)}, u32[]{:S(2)}) collective-permute-start(f32[2,1,32,128]{3,2,1,0:T(8,128)S(1)} %get-tuple-element.226), channel_id=1, source_target_pairs={{0,8},{8,16},{16,24},{24,32},{32,40},{40,48},{48,56},{56,64},{64,7... | collective-permute-start | bytes 98312 | tf_op jit(solution)/shard_map/while/body/eval_jaxpr/ppermute | solution.py:18
  58.1 6.5 %collective-permute-start = (f32[2,1,32,128]{3,2,1,0:T(8,128)S(1)}, f32[2,1,32,128]{3,2,1,0:T(8,128)S(1)}, u32[]{:S(2)}, u32[]{:S(2)}) collective-permute-start(f32[2,1,32,128]{3,2,1,0:T(8,128)S(1)} %get-tuple-element.225), channel_id=1, source_target_pairs={{8,0},{16,8},{24,16},{32,24},{40,32},{48,40},{56,48},{64,56},{72,6... | collective-permute-start | bytes 98312 | tf_op jit(solution)/shard_map/while/body/eval_jaxpr/ppermute | solution.py:21
  59.4 6.2 %collective-permute-start.1 = (f32[2,1,32,128]{3,2,1,0:T(8,128)S(1)}, f32[2,1,32,128]{3,2,1,0:T(8,128)S(1)}, u32[]{:S(2)}, u32[]{:S(2)}) collective-permute-start(f32[2,1,32,128]{3,2,1,0:T(8,128)S(1)} %get-tuple-element.226), channel_id=1, source_target_pairs={{0,8},{8,16},{16,24},{24,32},{32,40},{40,48},{48,56},{56,64},{64,7... | collective-permute-start | bytes 98312 | tf_op jit(solution)/shard_map/while/body/eval_jaxpr/ppermute | solution.py:18
  66.0 6.6 %collective-permute-start = (f32[2,1,32,128]{3,2,1,0:T(8,128)S(1)}, f32[2,1,32,128]{3,2,1,0:T(8,128)S(1)}, u32[]{:S(2)}, u32[]{:S(2)}) collective-permute-start(f32[2,1,32,128]{3,2,1,0:T(8,128)S(1)} %get-tuple-element.225), channel_id=1, source_target_pairs={{8,0},{16,8},{24,16},{32,24},{40,32},{48,40},{56,48},{64,56},{72,6... | collective-permute-start | bytes 98312 | tf_op jit(solution)/shard_map/while/body/eval_jaxpr/ppermute | solution.py:21
  67.3 6.3 %collective-permute-start.1 = (f32[2,1,32,128]{3,2,1,0:T(8,128)S(1)}, f32[2,1,32,128]{3,2,1,0:T(8,128)S(1)}, u32[]{:S(2)}, u32[]{:S(2)}) collective-permute-start(f32[2,1,32,128]{3,2,1,0:T(8,128)S(1)} %get-tuple-element.226), channel_id=1, source_target_pairs={{0,8},{8,16},{16,24},{24,32},{32,40},{40,48},{48,56},{56,64},{64,7... | collective-permute-start | bytes 98312 | tf_op jit(solution)/shard_map/while/body/eval_jaxpr/ppermute | solution.py:18
  74.1 6.7 %collective-permute-start = (f32[2,1,32,128]{3,2,1,0:T(8,128)S(1)}, f32[2,1,32,128]{3,2,1,0:T(8,128)S(1)}, u32[]{:S(2)}, u32[]{:S(2)}) collective-permute-start(f32[2,1,32,128]{3,2,1,0:T(8,128)S(1)} %get-tuple-element.225), channel_id=1, source_target_pairs={{8,0},{16,8},{24,16},{32,24},{40,32},{48,40},{56,48},{64,56},{72,6... | collective-permute-start | bytes 98312 | tf_op jit(solution)/shard_map/while/body/eval_jaxpr/ppermute | solution.py:21
  75.4 6.4 %collective-permute-start.1 = (f32[2,1,32,128]{3,2,1,0:T(8,128)S(1)}, f32[2,1,32,128]{3,2,1,0:T(8,128)S(1)}, u32[]{:S(2)}, u32[]{:S(2)}) collective-permute-start(f32[2,1,32,128]{3,2,1,0:T(8,128)S(1)} %get-tuple-element.226), channel_id=1, source_target_pairs={{0,8},{8,16},{16,24},{24,32},{32,40},{40,48},{48,56},{56,64},{64,7... | collective-permute-start | bytes 98312 | tf_op jit(solution)/shard_map/while/body/eval_jaxpr/ppermute | solution.py:18
  82.2 6.5 %collective-permute-start = (f32[2,1,32,128]{3,2,1,0:T(8,128)S(1)}, f32[2,1,32,128]{3,2,1,0:T(8,128)S(1)}, u32[]{:S(2)}, u32[]{:S(2)}) collective-permute-start(f32[2,1,32,128]{3,2,1,0:T(8,128)S(1)} %get-tuple-element.225), channel_id=1, source_target_pairs={{8,0},{16,8},{24,16},{32,24},{40,32},{48,40},{56,48},{64,56},{72,6... | collective-permute-start | bytes 98312 | tf_op jit(solution)/shard_map/while/body/eval_jaxpr/ppermute | solution.py:21
  83.5 6.2 %collective-permute-start.1 = (f32[2,1,32,128]{3,2,1,0:T(8,128)S(1)}, f32[2,1,32,128]{3,2,1,0:T(8,128)S(1)}, u32[]{:S(2)}, u32[]{:S(2)}) collective-permute-start(f32[2,1,32,128]{3,2,1,0:T(8,128)S(1)} %get-tuple-element.226), channel_id=1, source_target_pairs={{0,8},{8,16},{16,24},{24,32},{32,40},{40,48},{48,56},{56,64},{64,7... | collective-permute-start | bytes 98312 | tf_op jit(solution)/shard_map/while/body/eval_jaxpr/ppermute | solution.py:18
  90.2 7.9 %collective-permute-start = (f32[2,1,32,128]{3,2,1,0:T(8,128)S(1)}, f32[2,1,32,128]{3,2,1,0:T(8,128)S(1)}, u32[]{:S(2)}, u32[]{:S(2)}) collective-permute-start(f32[2,1,32,128]{3,2,1,0:T(8,128)S(1)} %get-tuple-element.225), channel_id=1, source_target_pairs={{8,0},{16,8},{24,16},{32,24},{40,32},{48,40},{56,48},{64,56},{72,6... | collective-permute-start | bytes 98312 | tf_op jit(solution)/shard_map/while/body/eval_jaxpr/ppermute | solution.py:21
  91.5 7.5 %collective-permute-start.1 = (f32[2,1,32,128]{3,2,1,0:T(8,128)S(1)}, f32[2,1,32,128]{3,2,1,0:T(8,128)S(1)}, u32[]{:S(2)}, u32[]{:S(2)}) collective-permute-start(f32[2,1,32,128]{3,2,1,0:T(8,128)S(1)} %get-tuple-element.226), channel_id=1, source_target_pairs={{0,8},{8,16},{16,24},{24,32},{32,40},{40,48},{48,56},{56,64},{64,7... | collective-permute-start | bytes 98312 | tf_op jit(solution)/shard_map/while/body/eval_jaxpr/ppermute | solution.py:18
  100.3 29.5 %all-to-all-start = ((f32[2,5,32,128]{3,0,1,2:T(2,128)}), f32[2,5,32,128]{3,0,1,2:T(2,128)S(1)}, u32[]{:S(2)}, u32[]{:S(2)}) async-start(f32[2,5,32,128]{3,0,1,2:T(2,128)} %copy.27), calls=%async_computation | async-start | bytes 327680 | tf_op jit(solution)/shard_map/all_to_all | solution.py:87
  129.8 0.7 copy-start
where the time goes:
time: 401 us; the launch traced here: 400 us
  blocking collectives  236 us (59%)
  starting transfers between devices  99.1 us (25%)
  other arithmetic  36.1 us (9%)
  waiting for transfers between devices  20.1 us (5%)
  local copies, waits for them, and re-layouts  7.41 us (2%)
    pmax x1, blocking collectives, body(): top_score = lax.pmax(local_top, ('space', 'sta'))  141 us
    psum x1, blocking collectives, body(): mass_sum = lax.psum(jnp.sum(cell_weights, 1), ('space', 'sta'))  94.4 us
    ppermute x12, starting transfers between devices, extended_2(): lax.ppermute(lax.slice_in_dim(block, block.shape[dim] - width, None, axis...  62.9 us
    all_to_all x1, starting transfers between devices, body(): lax.all_to_all(tables, 'sta', split_axis=2, concat_axis=0, tiled=True)  20.7 us
    ppermute x12, starting transfers between devices, extended_2(): lax.ppermute(lax.slice_in_dim(block, 0, width, axis=dim), axis, backward)  15.5 us
    reduce_sum x8, other arithmetic, misfit_block(): return jnp.sum(observed[:, :, None] * deviation * deviation, 1)  14 us
    ppermute x12, waiting for transfers between devices, extended_2(): lax.ppermute(lax.slice_in_dim(block, block.shape[dim] - width, None, axis...  11.5 us
    reduce_sum x8, other arithmetic, misfit_block(): jnp.sum(observed[:, :, None] * residual, 1) / pick_count[:, None]  9.54 us
  transfers between devices with their start and end apart: 25, of which 13 were waited for; matrix products, arithmetic and copies ran while one was open for 0% of the time, Pallas kernels for 0%

commit v1 on v0

--- a/solution.py
+++ b/solution.py
@@ -96,7 +96,9 @@
     local_top = jnp.max(score, 1)
     top_score = lax.pmax(local_top, ("space", "sta"))
     cell_weights = jnp.exp(score - top_score[:, None])
-    mass_sum = lax.psum(jnp.sum(cell_weights, 1), ("space", "sta"))
+    mass_sum = jnp.sum(cell_weights, 1)
+    for mesh_axis in ("sta", "space"):
+        mass_sum = lax.psum(mass_sum, mesh_axis)
     density = cell_weights / mass_sum[:, None]
     density = density.reshape(picks.shape[0], refined.shape[1], refined.shape[2], refined.shape[3])
     return (refined, density)

time: 401 us -> 475 us (1.18)
  the two profiles are of different devices: /device:TPU:1 before, /device:TPU:8 now
where the time goes in v1:
time: 475 us; the launch traced here: 474 us
  blocking collectives  308 us (65%)
  starting transfers between devices  90.2 us (19%)
  other arithmetic  36.1 us (8%)
  waiting for transfers between devices  29.7 us (6%)
  local copies, waits for them, and re-layouts  7.41 us (2%)
    psum x2, blocking collectives, body(): mass_sum = lax.psum(mass_sum, mesh_axis)  170 us
    pmax x1, blocking collectives, body(): top_score = lax.pmax(local_top, ('space', 'sta'))  138 us
    ppermute x12, starting transfers between devices, extended_2(): lax.ppermute(lax.slice_in_dim(block, block.shape[dim] - width, None, axis...  58 us
    ppermute x12, starting transfers between devices, extended_2(): lax.ppermute(lax.slice_in_dim(block, 0, width, axis=dim), axis, backward)  28.8 us
    ppermute x12, waiting for transfers between devices, extended_2(): lax.ppermute(lax.slice_in_dim(block, block.shape[dim] - width, None, axis...  20.5 us
    reduce_sum x8, other arithmetic, misfit_block(): return jnp.sum(observed[:, :, None] * deviation * deviation, 1)  14 us
    reduce_sum x8, other arithmetic, misfit_block(): jnp.sum(observed[:, :, None] * residual, 1) / pick_count[:, None]  9.54 us
  transfers between devices with their start and end apart: 25, of which 14 were waited for; matrix products, arithmetic and copies ran while one was open for 0% of the time, Pallas kernels for 0%

profile of v1, /device:TPU:8, one launch (start us, length us, event | category | flops | bytes accessed | tf_op | source)
XLA Modules:
  0.0 473.6 jit_solution(6114138409365929694)
XLA Ops:
  0.6 0.9 copy.54
  1.5 1.5 select_reduce_fusion
  3.1 114.0 %while.22 = (s32[]{:T(128)}, f32[2,5,32,128]{3,2,1,0:T(8,128)S(1)}, pred[]{:T(512)}, pred[]{:T(512)}, f32[5,32,128]{2,1,0:T(8,128)S(1)}, /*index=5*/f32[1,5,32,128]{3,2,1,0:T(8,128)S(1)}, s32[]{:T(128)}) while((s32[]{:T(128)}, f32[2,5,32,128]{3,2,1,0:T(8,128)S(1)}, pred[]{:T(512)}, pred[]{:T(512)}, f32[5,32,128]{2,1,0:T(8,128)S(1)}, ...), condition=%wide.region_2.3_spmd, body=%wide.region_1.2_spmd.sunk | while | flops 1523749 | bytes 2244781 | solution.py:86
  3.1 7.7 %collective-permute-start = (f32[2,1,32,128]{3,2,1,0:T(8,128)S(1)}, f32[2,1,32,128]{3,2,1,0:T(8,128)S(1)}, u32[]{:S(2)}, u32[]{:S(2)}) collective-permute-start(f32[2,1,32,128]{3,2,1,0:T(8,128)S(1)} %get-tuple-element.225), channel_id=1, source_target_pairs={{8,0},{16,8},{24,16},{32,24},{40,32},{48,40},{56,48},{64,56},{72,6... | collective-permute-start | bytes 98312 | tf_op jit(solution)/shard_map/while/body/eval_jaxpr/ppermute | solution.py:21
  10.8 1.9 collective-permute-start.1
  12.8 3.8 collective-permute-done.1
  17.1 1.9 collective-permute-start
  19.0 4.8 %collective-permute-start.1 = (f32[2,1,32,128]{3,2,1,0:T(8,128)S(1)}, f32[2,1,32,128]{3,2,1,0:T(8,128)S(1)}, u32[]{:S(2)}, u32[]{:S(2)}) collective-permute-start(f32[2,1,32,128]{3,2,1,0:T(8,128)S(1)} %get-tuple-element.226), channel_id=1, source_target_pairs={{0,8},{8,16},{16,24},{24,32},{32,40},{40,48},{48,56},{56,64},{64,7... | collective-permute-start | bytes 98312 | tf_op jit(solution)/shard_map/while/body/eval_jaxpr/ppermute | solution.py:18
  23.9 1.5 collective-permute-done.1
  25.9 1.9 collective-permute-start
  27.9 5.1 %collective-permute-start.1 = (f32[2,1,32,128]{3,2,1,0:T(8,128)S(1)}, f32[2,1,32,128]{3,2,1,0:T(8,128)S(1)}, u32[]{:S(2)}, u32[]{:S(2)}) collective-permute-start(f32[2,1,32,128]{3,2,1,0:T(8,128)S(1)} %get-tuple-element.226), channel_id=1, source_target_pairs={{0,8},{8,16},{16,24},{24,32},{32,40},{40,48},{48,56},{56,64},{64,7... | collective-permute-start | bytes 98312 | tf_op jit(solution)/shard_map/while/body/eval_jaxpr/ppermute | solution.py:18
  33.0 1.5 collective-permute-done.1
  35.0 1.9 collective-permute-start
  37.0 5.1 %collective-permute-start.1 = (f32[2,1,32,128]{3,2,1,0:T(8,128)S(1)}, f32[2,1,32,128]{3,2,1,0:T(8,128)S(1)}, u32[]{:S(2)}, u32[]{:S(2)}) collective-permute-start(f32[2,1,32,128]{3,2,1,0:T(8,128)S(1)} %get-tuple-element.226), channel_id=1, source_target_pairs={{0,8},{8,16},{16,24},{24,32},{32,40},{40,48},{48,56},{56,64},{64,7... | collective-permute-start | bytes 98312 | tf_op jit(solution)/shard_map/while/body/eval_jaxpr/ppermute | solution.py:18
  42.1 1.5 collective-permute-done.1
  44.2 1.9 collective-permute-start
  46.1 5.1 %collective-permute-start.1 = (f32[2,1,32,128]{3,2,1,0:T(8,128)S(1)}, f32[2,1,32,128]{3,2,1,0:T(8,128)S(1)}, u32[]{:S(2)}, u32[]{:S(2)}) collective-permute-start(f32[2,1,32,128]{3,2,1,0:T(8,128)S(1)} %get-tuple-element.226), channel_id=1, source_target_pairs={{0,8},{8,16},{16,24},{24,32},{32,40},{40,48},{48,56},{56,64},{64,7... | collective-permute-start | bytes 98312 | tf_op jit(solution)/shard_map/while/body/eval_jaxpr/ppermute | solution.py:18
  51.3 1.5 collective-permute-done.1
  53.3 1.9 collective-permute-start
  55.2 5.1 %collective-permute-start.1 = (f32[2,1,32,128]{3,2,1,0:T(8,128)S(1)}, f32[2,1,32,128]{3,2,1,0:T(8,128)S(1)}, u32[]{:S(2)}, u32[]{:S(2)}) collective-permute-start(f32[2,1,32,128]{3,2,1,0:T(8,128)S(1)} %get-tuple-element.226), channel_id=1, source_target_pairs={{0,8},{8,16},{16,24},{24,32},{32,40},{40,48},{48,56},{56,64},{64,7... | collective-permute-start | bytes 98312 | tf_op jit(solution)/shard_map/while/body/eval_jaxpr/ppermute | solution.py:18
  60.4 1.5 collective-permute-done.1
  62.4 1.9 collective-permute-start
  64.3 5.1 %collective-permute-start.1 = (f32[2,1,32,128]{3,2,1,0:T(8,128)S(1)}, f32[2,1,32,128]{3,2,1,0:T(8,128)S(1)}, u32[]{:S(2)}, u32[]{:S(2)}) collective-permute-start(f32[2,1,32,128]{3,2,1,0:T(8,128)S(1)} %get-tuple-element.226), channel_id=1, source_target_pairs={{0,8},{8,16},{16,24},{24,32},{32,40},{40,48},{48,56},{56,64},{64,7... | collective-permute-start | bytes 98312 | tf_op jit(solution)/shard_map/while/body/eval_jaxpr/ppermute | solution.py:18
  69.5 1.5 collective-permute-done.1
  71.5 1.9 collective-permute-start
  73.4 5.1 %collective-permute-start.1 = (f32[2,1,32,128]{3,2,1,0:T(8,128)S(1)}, f32[2,1,32,128]{3,2,1,0:T(8,128)S(1)}, u32[]{:S(2)}, u32[]{:S(2)}) collective-permute-start(f32[2,1,32,128]{3,2,1,0:T(8,128)S(1)} %get-tuple-element.226), channel_id=1, source_target_pairs={{0,8},{8,16},{16,24},{24,32},{32,40},{40,48},{48,56},{56,64},{64,7... | collective-permute-start | bytes 98312 | tf_op jit(solution)/shard_map/while/body/eval_jaxpr/ppermute | solution.py:18
  78.6 1.5 collective-permute-done.1
  80.6 1.9 collective-permute-start
  82.5 5.1 %collective-permute-start.1 = (f32[2,1,32,128]{3,2,1,0:T(8,128)S(1)}, f32[2,1,32,128]{3,2,1,0:T(8,128)S(1)}, u32[]{:S(2)}, u32[]{:S(2)}) collective-permute-start(f32[2,1,32,128]{3,2,1,0:T(8,128)S(1)} %get-tuple-element.226), channel_id=1, source_target_pairs={{0,8},{8,16},{16,24},{24,32},{32,40},{40,48},{48,56},{56,64},{64,7... | collective-permute-start | bytes 98312 | tf_op jit(solution)/shard_map/while/body/eval_jaxpr/ppermute | solution.py:18
  87.7 1.5 collective-permute-done.1
  89.7 1.9 collective-permute-start
  91.7 5.1 %collective-permute-start.1 = (f32[2,1,32,128]{3,2,1,0:T(8,128)S(1)}, f32[2,1,32,128]{3,2,1,0:T(8,128)S(1)}, u32[]{:S(2)}, u32[]{:S(2)}) collective-permute-start(f32[2,1,32,128]{3,2,1,0:T(8,128)S(1)} %get-tuple-element.226), channel_id=1, source_target_pairs={{0,8},{8,16},{16,24},{24,32},{32,40},{40,48},{48,56},{56,64},{64,7... | collective-permute-start | bytes 98312 | tf_op jit(solution)/shard_map/while/body/eval_jaxpr/ppermute | solution.py:18
  97.0 1.4 collective-permute-done.1
  98.9 1.9 collective-permute-start
  100.8 5.1 %collective-permute-start.1 = (f32[2,1,32,128]{3,2,1,0:T(8,128)S(1)}, f32[2,1,32,128]{3,2,1,0:T(8,128)S(1)}, u32[]{:S(2)}, u32[]{:S(2)}) collective-permute-start(f32[2,1,32,128]{3,2,1,0:T(8,128)S(1)} %get-tuple-element.226), channel_id=1, source_target_pairs={{0,8},{8,16},{16,24},{24,32},{32,40},{40,48},{48,56},{56,64},{64,7... | collective-permute-start | bytes 98312 | tf_op jit(solution)/shard_map/while/body/eval_jaxpr/ppermute | solution.py:18
  106.0 1.5 collective-permute-done.1
  108.0 1.9 collective-permute-start
  109.9 5.1 %collective-permute-start.1 = (f32[2,1,32,128]{3,2,1,0:T(8,128)S(1)}, f32[2,1,32,128]{3,2,1,0:T(8,128)S(1)}, u32[]{:S(2)}, u32[]{:S(2)}) collective-permute-start(f32[2,1,32,128]{3,2,1,0:T(8,128)S(1)} %get-tuple-element.226), channel_id=1, source_target_pairs={{0,8},{8,16},{16,24},{24,32},{32,40},{40,48},{48,56},{56,64},{64,7... | collective-permute-start | bytes 98312 | tf_op jit(solution)/shard_map/while/body/eval_jaxpr/ppermute | solution.py:18
  115.1 1.5 collective-permute-done.1
  117.9 3.4 all-to-all-start
  121.4 9.0 %all-to-all-done = f32[2,5,32,128]{3,0,1,2:T(2,128)S(1)} async-done(((f32[2,5,32,128]{3,0,1,2:T(2,128)}), f32[2,5,32,128]{3,0,1,2:T(2,128)S(1)}, u32[]{:S(2)}, u32[]{:S(2)}) %all-to-all-start) | async-done | bytes 163872 | tf_op jit(solution)/shard_map/all_to_all | solution.py:87
  131.1 26.5 %while.23 = (s32[]{:T(128)}, f32[8,32,2560]{2,1,0:T(8,128)S(1)}, f32[8,32,16]{1,0,2:T(8,128)S(1)}, f32[8,32,16]{1,0,2:T(8,128)S(1)}, f32[16,5,4,128]{3,2,1,0:T(4...) while((s32[]{:T(128)}, f32[8,32,2560]{2,1,0:T(8,128)S(1)}, f32[8,32,16]{1,0,2:T(8,128)S(1)}, ...), condition=%wide.wide.region_7.8_spmd, body=%wide.wide.region_3.7_spmd.sunk | while | flops 10404322 | bytes 2648417 | solution.py:91
  131.3 1.2 fusion.17
  132.6 1.8 fusion.18
  134.6 1.2 fusion.17
  135.9 1.8 fusion.18
  137.9 1.2 fusion.17
  139.2 1.8 fusion.18
  141.2 1.2 fusion.17
  142.5 1.8 fusion.18
  144.5 1.2 fusion.17
  145.9 1.8 fusion.18
  147.8 1.2 fusion.17
  149.2 1.8 fusion.18
  151.2 1.2 fusion.17
  152.5 1.8 fusion.18
  154.5 1.2 fusion.17
  155.8 1.8 fusion.18
  157.9 138.1 %pmax.7 = f32[256]{0:T(256)S(1)} all-reduce(f32[256]{0:T(256)S(1)} %reduce_max.12), channel_id=1, replica_groups=mesh['space'=64,'sta'=8] {'space','sta'}, use_global_device_ids=true, to_apply=%region_9.10 | all-reduce | flops 256 | bytes 2048 | tf_op jit(solution)/shard_map/pmax | solution.py:97
  296.1 2.0 exponential_reduce_fusion
  298.1 2.8 div.34
  301.0 16.3 %psum.14 = f32[256]{0:T(256)S(1)} all-reduce(f32[256]{0:T(256)S(1)} %reduce_sum.49), channel_id=1, replica_groups=mesh['space'=64,'sta'=8] {'sta'}, use_global_device_ids=true, to_apply=%region_11.12 | all-reduce | flops 256 | bytes 2048 | tf_op jit(solution)/shard_map/psum | solution.py:101
  317.3 153.7 %psum.15 = f32[256]{0:T(256)S(1)} all-reduce(f32[256]{0:T(256)S(1)} %psum.14), channel_id=1, replica_groups=mesh['space'=64,'sta'=8] {'space'}, use_global_device_ids=true, to_apply=%region_12.13 | all-reduce | flops 256 | bytes 2048 | tf_op jit(solution)/shard_map/psum | solution.py:101
  471.0 2.5 exponential_divide_fusion
  (150 shorter events, 10.3 us)
Async XLA Ops:
  3.1 118.2 %copy-start.2 = (s32[256,16]{0,1:T(8,128)S(1)}, s32[256,16]{0,1:T(8,128)}, u32[]{:S(2)}) copy-start(s32[256,16]{0,1:T(8,128)} %param.13) | copy-start | bytes 49156
  3.1 118.3 %copy-start.1 = (f32[256,16]{0,1:T(8,128)S(1)}, f32[256,16]{0,1:T(8,128)}, u32[]{:S(2)}) copy-start(f32[256,16]{0,1:T(8,128)} %param.12) | copy-start | bytes 49156
  3.1 9.7 %collective-permute-start = (f32[2,1,32,128]{3,2,1,0:T(8,128)S(1)}, f32[2,1,32,128]{3,2,1,0:T(8,128)S(1)}, u32[]{:S(2)}, u32[]{:S(2)}) collective-permute-start(f32[2,1,32,128]{3,2,1,0:T(8,128)S(1)} %get-tuple-element.225), channel_id=1, source_target_pairs={{8,0},{16,8},{24,16},{32,24},{40,32},{48,40},{56,48},{64,56},{72,6... | collective-permute-start | bytes 98312 | tf_op jit(solution)/shard_map/while/body/eval_jaxpr/ppermute | solution.py:21
  10.8 5.8 %collective-permute-start.1 = (f32[2,1,32,128]{3,2,1,0:T(8,128)S(1)}, f32[2,1,32,128]{3,2,1,0:T(8,128)S(1)}, u32[]{:S(2)}, u32[]{:S(2)}) collective-permute-start(f32[2,1,32,128]{3,2,1,0:T(8,128)S(1)} %get-tuple-element.226), channel_id=1, source_target_pairs={{0,8},{8,16},{16,24},{24,32},{32,40},{40,48},{48,56},{56,64},{64,7... | collective-permute-start | bytes 98312 | tf_op jit(solution)/shard_map/while/body/eval_jaxpr/ppermute | solution.py:18
  17.1 6.8 %collective-permute-start = (f32[2,1,32,128]{3,2,1,0:T(8,128)S(1)}, f32[2,1,32,128]{3,2,1,0:T(8,128)S(1)}, u32[]{:S(2)}, u32[]{:S(2)}) collective-permute-start(f32[2,1,32,128]{3,2,1,0:T(8,128)S(1)} %get-tuple-element.225), channel_id=1, source_target_pairs={{8,0},{16,8},{24,16},{32,24},{40,32},{48,40},{56,48},{64,56},{72,6... | collective-permute-start | bytes 98312 | tf_op jit(solution)/shard_map/while/body/eval_jaxpr/ppermute | solution.py:21
  19.0 6.4 %collective-permute-start.1 = (f32[2,1,32,128]{3,2,1,0:T(8,128)S(1)}, f32[2,1,32,128]{3,2,1,0:T(8,128)S(1)}, u32[]{:S(2)}, u32[]{:S(2)}) collective-permute-start(f32[2,1,32,128]{3,2,1,0:T(8,128)S(1)} %get-tuple-element.226), channel_id=1, source_target_pairs={{0,8},{8,16},{16,24},{24,32},{32,40},{40,48},{48,56},{56,64},{64,7... | collective-permute-start | bytes 98312 | tf_op jit(solution)/shard_map/while/body/eval_jaxpr/ppermute | solution.py:18
  25.9 7.1 %collective-permute-start = (f32[2,1,32,128]{3,2,1,0:T(8,128)S(1)}, f32[2,1,32,128]{3,2,1,0:T(8,128)S(1)}, u32[]{:S(2)}, u32[]{:S(2)}) collective-permute-start(f32[2,1,32,128]{3,2,1,0:T(8,128)S(1)} %get-tuple-element.225), channel_id=1, source_target_pairs={{8,0},{16,8},{24,16},{32,24},{40,32},{48,40},{56,48},{64,56},{72,6... | collective-permute-start | bytes 98312 | tf_op jit(solution)/shard_map/while/body/eval_jaxpr/ppermute | solution.py:21
  27.9 6.7 %collective-permute-start.1 = (f32[2,1,32,128]{3,2,1,0:T(8,128)S(1)}, f32[2,1,32,128]{3,2,1,0:T(8,128)S(1)}, u32[]{:S(2)}, u32[]{:S(2)}) collective-permute-start(f32[2,1,32,128]{3,2,1,0:T(8,128)S(1)} %get-tuple-element.226), channel_id=1, source_target_pairs={{0,8},{8,16},{16,24},{24,32},{32,40},{40,48},{48,56},{56,64},{64,7... | collective-permute-start | bytes 98312 | tf_op jit(solution)/shard_map/while/body/eval_jaxpr/ppermute | solution.py:18
  35.0 7.1 %collective-permute-start = (f32[2,1,32,128]{3,2,1,0:T(8,128)S(1)}, f32[2,1,32,128]{3,2,1,0:T(8,128)S(1)}, u32[]{:S(2)}, u32[]{:S(2)}) collective-permute-start(f32[2,1,32,128]{3,2,1,0:T(8,128)S(1)} %get-tuple-element.225), channel_id=1, source_target_pairs={{8,0},{16,8},{24,16},{32,24},{40,32},{48,40},{56,48},{64,56},{72,6... | collective-permute-start | bytes 98312 | tf_op jit(solution)/shard_map/while/body/eval_jaxpr/ppermute | solution.py:21
  37.0 6.7 %collective-permute-start.1 = (f32[2,1,32,128]{3,2,1,0:T(8,128)S(1)}, f32[2,1,32,128]{3,2,1,0:T(8,128)S(1)}, u32[]{:S(2)}, u32[]{:S(2)}) collective-permute-start(f32[2,1,32,128]{3,2,1,0:T(8,128)S(1)} %get-tuple-element.226), channel_id=1, source_target_pairs={{0,8},{8,16},{16,24},{24,32},{32,40},{40,48},{48,56},{56,64},{64,7... | collective-permute-start | bytes 98312 | tf_op jit(solution)/shard_map/while/body/eval_jaxpr/ppermute | solution.py:18
  44.2 7.1 %collective-permute-start = (f32[2,1,32,128]{3,2,1,0:T(8,128)S(1)}, f32[2,1,32,128]{3,2,1,0:T(8,128)S(1)}, u32[]{:S(2)}, u32[]{:S(2)}) collective-permute-start(f32[2,1,32,128]{3,2,1,0:T(8,128)S(1)} %get-tuple-element.225), channel_id=1, source_target_pairs={{8,0},{16,8},{24,16},{32,24},{40,32},{48,40},{56,48},{64,56},{72,6... | collective-permute-start | bytes 98312 | tf_op jit(solution)/shard_map/while/body/eval_jaxpr/ppermute | solution.py:21
  46.1 6.7 %collective-permute-start.1 = (f32[2,1,32,128]{3,2,1,0:T(8,128)S(1)}, f32[2,1,32,128]{3,2,1,0:T(8,128)S(1)}, u32[]{:S(2)}, u32[]{:S(2)}) collective-permute-start(f32[2,1,32,128]{3,2,1,0:T(8,128)S(1)} %get-tuple-element.226), channel_id=1, source_target_pairs={{0,8},{8,16},{16,24},{24,32},{32,40},{40,48},{48,56},{56,64},{64,7... | collective-permute-start | bytes 98312 | tf_op jit(solution)/shard_map/while/body/eval_jaxpr/ppermute | solution.py:18
  53.3 7.1 %collective-permute-start = (f32[2,1,32,128]{3,2,1,0:T(8,128)S(1)}, f32[2,1,32,128]{3,2,1,0:T(8,128)S(1)}, u32[]{:S(2)}, u32[]{:S(2)}) collective-permute-start(f32[2,1,32,128]{3,2,1,0:T(8,128)S(1)} %get-tuple-element.225), channel_id=1, source_target_pairs={{8,0},{16,8},{24,16},{32,24},{40,32},{48,40},{56,48},{64,56},{72,6... | collective-permute-start | bytes 98312 | tf_op jit(solution)/shard_map/while/body/eval_jaxpr/ppermute | solution.py:21
  55.2 6.7 %collective-permute-start.1 = (f32[2,1,32,128]{3,2,1,0:T(8,128)S(1)}, f32[2,1,32,128]{3,2,1,0:T(8,128)S(1)}, u32[]{:S(2)}, u32[]{:S(2)}) collective-permute-start(f32[2,1,32,128]{3,2,1,0:T(8,128)S(1)} %get-tuple-element.226), channel_id=1, source_target_pairs={{0,8},{8,16},{16,24},{24,32},{32,40},{40,48},{48,56},{56,64},{64,7... | collective-permute-start | bytes 98312 | tf_op jit(solution)/shard_map/while/body/eval_jaxpr/ppermute | solution.py:18
  62.4 7.1 %collective-permute-start = (f32[2,1,32,128]{3,2,1,0:T(8,128)S(1)}, f32[2,1,32,128]{3,2,1,0:T(8,128)S(1)}, u32[]{:S(2)}, u32[]{:S(2)}) collective-permute-start(f32[2,1,32,128]{3,2,1,0:T(8,128)S(1)} %get-tuple-element.225), channel_id=1, source_target_pairs={{8,0},{16,8},{24,16},{32,24},{40,32},{48,40},{56,48},{64,56},{72,6... | collective-permute-start | bytes 98312 | tf_op jit(solution)/shard_map/while/body/eval_jaxpr/ppermute | solution.py:21
  64.3 6.7 %collective-permute-start.1 = (f32[2,1,32,128]{3,2,1,0:T(8,128)S(1)}, f32[2,1,32,128]{3,2,1,0:T(8,128)S(1)}, u32[]{:S(2)}, u32[]{:S(2)}) collective-permute-start(f32[2,1,32,128]{3,2,1,0:T(8,128)S(1)} %get-tuple-element.226), channel_id=1, source_target_pairs={{0,8},{8,16},{16,24},{24,32},{32,40},{40,48},{48,56},{56,64},{64,7... | collective-permute-start | bytes 98312 | tf_op jit(solution)/shard_map/while/body/eval_jaxpr/ppermute | solution.py:18
  71.5 7.1 %collective-permute-start = (f32[2,1,32,128]{3,2,1,0:T(8,128)S(1)}, f32[2,1,32,128]{3,2,1,0:T(8,128)S(1)}, u32[]{:S(2)}, u32[]{:S(2)}) collective-permute-start(f32[2,1,32,128]{3,2,1,0:T(8,128)S(1)} %get-tuple-element.225), channel_id=1, source_target_pairs={{8,0},{16,8},{24,16},{32,24},{40,32},{48,40},{56,48},{64,56},{72,6... | collective-permute-start | bytes 98312 | tf_op jit(solution)/shard_map/while/body/eval_jaxpr/ppermute | solution.py:21
  73.4 6.7 %collective-permute-start.1 = (f32[2,1,32,128]{3,2,1,0:T(8,128)S(1)}, f32[2,1,32,128]{3,2,1,0:T(8,128)S(1)}, u32[]{:S(2)}, u32[]{:S(2)}) collective-permute-start(f32[2,1,32,128]{3,2,1,0:T(8,128)S(1)} %get-tuple-element.226), channel_id=1, source_target_pairs={{0,8},{8,16},{16,24},{24,32},{32,40},{40,48},{48,56},{56,64},{64,7... | collective-permute-start | bytes 98312 | tf_op jit(solution)/shard_map/while/body/eval_jaxpr/ppermute | solution.py:18
  80.6 7.1 %collective-permute-start = (f32[2,1,32,128]{3,2,1,0:T(8,128)S(1)}, f32[2,1,32,128]{3,2,1,0:T(8,128)S(1)}, u32[]{:S(2)}, u32[]{:S(2)}) collective-permute-start(f32[2,1,32,128]{3,2,1,0:T(8,128)S(1)} %get-tuple-element.225), channel_id=1, source_target_pairs={{8,0},{16,8},{24,16},{32,24},{40,32},{48,40},{56,48},{64,56},{72,6... | collective-permute-start | bytes 98312 | tf_op jit(solution)/shard_map/while/body/eval_jaxpr/ppermute | solution.py:21
  82.5 6.7 %collective-permute-start.1 = (f32[2,1,32,128]{3,2,1,0:T(8,128)S(1)}, f32[2,1,32,128]{3,2,1,0:T(8,128)S(1)}, u32[]{:S(2)}, u32[]{:S(2)}) collective-permute-start(f32[2,1,32,128]{3,2,1,0:T(8,128)S(1)} %get-tuple-element.226), channel_id=1, source_target_pairs={{0,8},{8,16},{16,24},{24,32},{32,40},{40,48},{48,56},{56,64},{64,7... | collective-permute-start | bytes 98312 | tf_op jit(solution)/shard_map/while/body/eval_jaxpr/ppermute | solution.py:18
  89.7 7.2 %collective-permute-start = (f32[2,1,32,128]{3,2,1,0:T(8,128)S(1)}, f32[2,1,32,128]{3,2,1,0:T(8,128)S(1)}, u32[]{:S(2)}, u32[]{:S(2)}) collective-permute-start(f32[2,1,32,128]{3,2,1,0:T(8,128)S(1)} %get-tuple-element.225), channel_id=1, source_target_pairs={{8,0},{16,8},{24,16},{32,24},{40,32},{48,40},{56,48},{64,56},{72,6... | collective-permute-start | bytes 98312 | tf_op jit(solution)/shard_map/while/body/eval_jaxpr/ppermute | solution.py:21
  91.7 6.7 %collective-permute-start.1 = (f32[2,1,32,128]{3,2,1,0:T(8,128)S(1)}, f32[2,1,32,128]{3,2,1,0:T(8,128)S(1)}, u32[]{:S(2)}, u32[]{:S(2)}) collective-permute-start(f32[2,1,32,128]{3,2,1,0:T(8,128)S(1)} %get-tuple-element.226), channel_id=1, source_target_pairs={{0,8},{8,16},{16,24},{24,32},{32,40},{40,48},{48,56},{56,64},{64,7... | collective-permute-start | bytes 98312 | tf_op jit(solution)/shard_map/while/body/eval_jaxpr/ppermute | solution.py:18
  98.9 7.1 %collective-permute-start = (f32[2,1,32,128]{3,2,1,0:T(8,128)S(1)}, f32[2,1,32,128]{3,2,1,0:T(8,128)S(1)}, u32[]{:S(2)}, u32[]{:S(2)}) collective-permute-start(f32[2,1,32,128]{3,2,1,0:T(8,128)S(1)} %get-tuple-element.225), channel_id=1, source_target_pairs={{8,0},{16,8},{24,16},{32,24},{40,32},{48,40},{56,48},{64,56},{72,6... | collective-permute-start | bytes 98312 | tf_op jit(solution)/shard_map/while/body/eval_jaxpr/ppermute | solution.py:21
  100.8 6.7 %collective-permute-start.1 = (f32[2,1,32,128]{3,2,1,0:T(8,128)S(1)}, f32[2,1,32,128]{3,2,1,0:T(8,128)S(1)}, u32[]{:S(2)}, u32[]{:S(2)}) collective-permute-start(f32[2,1,32,128]{3,2,1,0:T(8,128)S(1)} %get-tuple-element.226), channel_id=1, source_target_pairs={{0,8},{8,16},{16,24},{24,32},{32,40},{40,48},{48,56},{56,64},{64,7... | collective-permute-start | bytes 98312 | tf_op jit(solution)/shard_map/while/body/eval_jaxpr/ppermute | solution.py:18
  108.0 7.1 %collective-permute-start = (f32[2,1,32,128]{3,2,1,0:T(8,128)S(1)}, f32[2,1,32,128]{3,2,1,0:T(8,128)S(1)}, u32[]{:S(2)}, u32[]{:S(2)}) collective-permute-start(f32[2,1,32,128]{3,2,1,0:T(8,128)S(1)} %get-tuple-element.225), channel_id=1, source_target_pairs={{8,0},{16,8},{24,16},{32,24},{40,32},{48,40},{56,48},{64,56},{72,6... | collective-permute-start | bytes 98312 | tf_op jit(solution)/shard_map/while/body/eval_jaxpr/ppermute | solution.py:21
  109.9 6.7 %collective-permute-start.1 = (f32[2,1,32,128]{3,2,1,0:T(8,128)S(1)}, f32[2,1,32,128]{3,2,1,0:T(8,128)S(1)}, u32[]{:S(2)}, u32[]{:S(2)}) collective-permute-start(f32[2,1,32,128]{3,2,1,0:T(8,128)S(1)} %get-tuple-element.226), channel_id=1, source_target_pairs={{0,8},{8,16},{16,24},{24,32},{32,40},{40,48},{48,56},{56,64},{64,7... | collective-permute-start | bytes 98312 | tf_op jit(solution)/shard_map/while/body/eval_jaxpr/ppermute | solution.py:18
  117.9 12.5 %all-to-all-start = ((f32[2,5,32,128]{3,0,1,2:T(2,128)}), f32[2,5,32,128]{3,0,1,2:T(2,128)S(1)}, u32[]{:S(2)}, u32[]{:S(2)}) async-start(f32[2,5,32,128]{3,0,1,2:T(2,128)} %copy.27), calls=%async_computation | async-start | bytes 327680 | tf_op jit(solution)/shard_map/all_to_all | solution.py:87
  130.4 0.7 copy-start
